TPU v7x, 32 devices: a whole 2x2x4 slice. The times are simulated.
32 devices in a mesh: dp: 8 (over z, core), tensor: 4 (over y, x).
Axes of the slice: x: 2, y: 2, z: 4, core: 2. Of those that a mesh axis runs over, the one named last changes fastest.
Arguments:
- tokens: bfloat16 [8192, 2048], P('dp'), may hold values from -6 to 6
- cotangent: bfloat16 [8192, 2048], P('dp'), may hold values from -6 to 6
- seq_lengths: int32 [4], replicated, may hold values from 1536 to 2048, as said below
- slot_seq: int32 [4], replicated, may hold values from 0 to 3, each once
- w_query: float32 [2048, 2048], P('dp', 'tensor'), may hold values from -0.125 to 0.125
- w_key: float32 [2048, 2048], P('dp', 'tensor'), may hold values from -0.125 to 0.125
- w_value: float32 [2048, 2048], P('dp', 'tensor'), may hold values from -0.125 to 0.125
- b_query: float32 [2048], P('tensor'), may hold values from -3 to 3
- b_value: float32 [2048], P('tensor'), may hold values from -3 to 3
- w_out: float32 [2048, 2048], P('tensor', 'dp'), may hold values from -4 to 4
- b_out: float32 [2048], replicated, may hold values from -3 to 3
- ln1_gain: float32 [2048], replicated, may hold values from 0.5 to 1.5
- ln1_bias: float32 [2048], replicated, may hold values from -3 to 3
- w_inner: float32 [2048, 8192], P('dp', 'tensor'), may hold values from -0.125 to 0.125
- b_inner: float32 [8192], P('tensor'), may hold values from -3 to 3
- w_outer: float32 [8192, 2048], P('tensor', 'dp'), may hold values from -0.0625 to 0.0625
- b_outer: float32 [2048], replicated, may hold values from -3 to 3
- ln2_gain: float32 [2048], replicated, may hold values from 0.5 to 1.5
- ln2_bias: float32 [2048], replicated, may hold values from -3 to 3
Outputs:
- output: float32 [8192, 2048], P('dp')
- grad_tokens: float32 [8192, 2048], P('dp')
- grad_w_query: float32 [2048, 2048], P('dp', 'tensor')
- grad_w_key: float32 [2048, 2048], P('dp', 'tensor')
- grad_w_value: float32 [2048, 2048], P('dp', 'tensor')
- grad_b_query: float32 [2048], P('tensor')
- grad_b_value: float32 [2048], P('tensor')
- grad_w_out: float32 [2048, 2048], P('tensor', 'dp')
- grad_b_out: float32 [2048], replicated
- grad_ln1_gain: float32 [2048], replicated
- grad_ln1_bias: float32 [2048], replicated
- grad_w_inner: float32 [2048, 8192], P('dp', 'tensor')
- grad_b_inner: float32 [8192], P('tensor')
- grad_w_outer: float32 [8192, 2048], P('tensor', 'dp')
- grad_b_outer: float32 [2048], replicated
- grad_ln2_gain: float32 [2048], replicated
- grad_ln2_bias: float32 [2048], replicated
Inputs may be any that keep to these rules, and one draw needn't show every extreme that they name: `seq_lengths`: each sequence's valid tokens; some sequence has exactly 2048 and some exactly 1536. `slot_seq`: each sequence stands in exactly one slot.
All inputs are finite; a program needn't handle non-finite values.
Results may differ from a plain program's by a relative error of at most 0.019.
Values may be sent and summed in bfloat16 or wider, within the bound.
No kernel may reach another device: no remote copies, remote signals or barrier semaphores. Data moves between devices by JAX's collectives and lax.ppermute only.
A program may use at most 256 MiB of HBM per device.

v0:
```python
import jax
import jax.numpy as jnp
from jax import lax
from jax.sharding import PartitionSpec as P

HEAD_DIM = 128
SLOT = 2048
norm_eps = 1e-12


def passed_along(value, axis, steps):
    count = lax.axis_size(axis)
    leading, last = (max(0, -steps), min(count, count - steps))
    return lax.ppermute(value, axis, [(source, source + steps) for source in range(leading, last)])


def layer_norm(resid, gain, shift):
    center = resid - jnp.mean(resid, axis=-1, keepdims=True)
    spread = jnp.mean(center * center, axis=-1, keepdims=True)
    return center * lax.rsqrt(spread + norm_eps) * gain + shift


def gelu_tanh(inner):
    return 0.5 * inner * (1.0 + jnp.tanh(0.7978845608 * (inner + 0.044715 * inner * inner * inner)))


def mat_bf(left, right):
    return jnp.dot(left, right, preferred_element_type=jnp.float32)


def tensor_total(part):
    return lax.psum(part, "tensor")


def on_device(
    tokens,
    cotangent,
    seq_lengths,
    slot_seq,
    w_query,
    w_key,
    w_value,
    b_query,
    b_value,
    w_out,
    b_out,
    ln1_gain,
    ln1_bias,
    w_inner,
    b_inner,
    w_outer,
    b_outer,
    ln2_gain,
    ln2_bias,
):
    tok_rows = tokens.shape[0]
    shard_count = SLOT // tok_rows
    width_here = w_query.shape[1]
    heads_here = width_here // HEAD_DIM
    score_scale = HEAD_DIM ** (-0.5)
    block_rows = min(512, tok_rows)
    block_count = tok_rows // block_rows
    dp_place = lax.axis_index("dp")
    my_slot = dp_place // shard_count
    my_spot = dp_place % shard_count
    slot_ids = jnp.arange(slot_seq.shape[0])
    slot_lengths = jnp.sum(
        jnp.where(slot_seq[:, None] == slot_ids[None, :], seq_lengths[None, :], 0), axis=1
    )
    my_length = jnp.sum(jnp.where(slot_ids == my_slot, slot_lengths, 0))
    row_live = (my_spot * tok_rows + jnp.arange(tok_rows) < my_length).astype(jnp.float32)
    key_live = jnp.arange(SLOT) < my_length
    spot_ids = jnp.arange(shard_count)
    offset_list = [step_by for step_by in range(1 - shard_count, shard_count) if step_by != 0]
    own_hit = (spot_ids == my_spot)[:, None, None]
    tokens_wide = tokens.astype(jnp.float32)
    cot_wide = cotangent.astype(jnp.float32)
    full_query, full_key, full_value, full_out = (
        lax.all_gather(w_query.astype(jnp.bfloat16), "dp", axis=0, tiled=True),
        lax.all_gather(w_key.astype(jnp.bfloat16), "dp", axis=0, tiled=True),
        lax.all_gather(w_value.astype(jnp.bfloat16), "dp", axis=0, tiled=True),
        lax.all_gather(w_out.astype(jnp.bfloat16), "dp", axis=1, tiled=True),
    )
    query_rows = (mat_bf(tokens, full_query) + b_query).astype(jnp.bfloat16)
    key_rows = mat_bf(tokens, full_key).astype(jnp.bfloat16)
    value_rows = (mat_bf(tokens, full_value) + b_value).astype(jnp.bfloat16)
    empty_slab = jnp.zeros((shard_count, tok_rows, width_here), jnp.bfloat16)
    key_slab = jnp.where(own_hit, key_rows[None], empty_slab)
    value_slab = jnp.where(own_hit, value_rows[None], empty_slab)
    for step_by in offset_list:
        far_key, far_value = passed_along((key_rows, value_rows), "dp", step_by)
        far_hit = (spot_ids == my_spot - step_by)[:, None, None]
        key_slab = jnp.where(far_hit, far_key[None], key_slab)
        value_slab = jnp.where(far_hit, far_value[None], value_slab)
    slot_keys = key_slab.reshape(SLOT, heads_here, HEAD_DIM)
    slot_values = value_slab.reshape(SLOT, heads_here, HEAD_DIM)
    query_blocks = query_rows.reshape(block_count, block_rows, heads_here, HEAD_DIM)

    def score_block(query_part):
        scores = (
            jnp.einsum("qhd,khd->hqk", query_part, slot_keys, preferred_element_type=jnp.float32)
            * score_scale
        )
        return jnp.where(key_live[None, None, :], scores, -1e30)

    def forward_block(query_part):
        scores = score_block(query_part)
        top = jnp.max(scores, axis=-1, keepdims=True)
        expd = jnp.exp(scores - top)
        total = jnp.sum(expd, axis=-1, keepdims=True)
        probs = expd / total
        mixed = jnp.einsum(
            "hqk,khd->qhd",
            probs.astype(jnp.bfloat16),
            slot_values,
            preferred_element_type=jnp.float32,
        )
        return (mixed, top + jnp.log(total))

    mixed_blocks, lse_blocks = lax.map(forward_block, query_blocks)
    heads_rows = mixed_blocks.reshape(tok_rows, width_here).astype(jnp.bfloat16)
    attn_part = mat_bf(heads_rows, full_out)
    attn = tensor_total(attn_part) + b_out
    resid_one = tokens_wide + attn
    hidden, norm_one_back = jax.vjp(layer_norm, resid_one, ln1_gain, ln1_bias)
    hidden_low = hidden.astype(jnp.bfloat16)
    full_inner, full_outer = (
        lax.all_gather(w_inner.astype(jnp.bfloat16), "dp", axis=0, tiled=True),
        lax.all_gather(w_outer.astype(jnp.bfloat16), "dp", axis=1, tiled=True),
    )
    inner = mat_bf(hidden_low, full_inner) + b_inner
    act_low = gelu_tanh(inner).astype(jnp.bfloat16)
    outer_part = mat_bf(act_low, full_outer)
    outer = tensor_total(outer_part) + b_outer
    output, norm_two_back = jax.vjp(layer_norm, hidden + outer, ln2_gain, ln2_bias)
    grad_out = cot_wide * row_live[:, None]
    grad_two, grad_ln2_gain, grad_ln2_bias = norm_two_back(grad_out)
    back_inner, back_outer = (
        lax.all_gather(w_inner.astype(jnp.bfloat16), "dp", axis=0, tiled=True),
        lax.all_gather(w_outer.astype(jnp.bfloat16), "dp", axis=1, tiled=True),
    )
    outer_low = grad_two.astype(jnp.bfloat16)
    grad_b_outer = jnp.sum(grad_two, axis=0)
    grad_w_outer = jnp.einsum("tf,td->fd", act_low, outer_low, preferred_element_type=jnp.float32)
    grad_act = jnp.einsum("td,fd->tf", outer_low, back_outer, preferred_element_type=jnp.float32)
    gelu_value, gelu_back = jax.vjp(gelu_tanh, inner)
    inner_low = gelu_back(grad_act)[0].astype(jnp.bfloat16)
    grad_b_inner = jnp.sum(inner_low.astype(jnp.float32), axis=0)
    grad_w_inner = jnp.einsum(
        "td,tf->df", hidden_low, inner_low, preferred_element_type=jnp.float32
    )
    grad_w_inner, grad_w_outer = (
        lax.psum_scatter(
            grad_w_inner.astype(jnp.bfloat16), "dp", scatter_dimension=0, tiled=True
        ).astype(jnp.float32),
        lax.psum_scatter(
            grad_w_outer.astype(jnp.bfloat16), "dp", scatter_dimension=1, tiled=True
        ).astype(jnp.float32),
    )
    hidden_part = jnp.einsum("tf,df->td", inner_low, back_inner, preferred_element_type=jnp.float32)
    grad_hidden = grad_two + tensor_total(hidden_part)
    grad_one, grad_ln1_gain, grad_ln1_bias = norm_one_back(grad_hidden)
    attn_low = grad_one.astype(jnp.bfloat16)
    grad_b_out = jnp.sum(grad_one, axis=0)
    back_query, back_key, back_value, back_out = (
        lax.all_gather(w_query.astype(jnp.bfloat16), "dp", axis=0, tiled=True),
        lax.all_gather(w_key.astype(jnp.bfloat16), "dp", axis=0, tiled=True),
        lax.all_gather(w_value.astype(jnp.bfloat16), "dp", axis=0, tiled=True),
        lax.all_gather(w_out.astype(jnp.bfloat16), "dp", axis=1, tiled=True),
    )
    grad_w_out = jnp.einsum("tc,td->cd", heads_rows, attn_low, preferred_element_type=jnp.float32)
    mixed_low = jnp.einsum(
        "td,cd->tc", attn_low, back_out, preferred_element_type=jnp.float32
    ).astype(jnp.bfloat16)
    grad_blocks = mixed_low.reshape(block_count, block_rows, heads_here, HEAD_DIM)

    def backward_block(carry, inputs):
        key_sum, value_sum = carry
        query_part, grad_part, lse_part = inputs
        probs = jnp.exp(score_block(query_part) - lse_part)
        grad_probs = jnp.einsum(
            "qhd,khd->hqk", grad_part, slot_values, preferred_element_type=jnp.float32
        )
        inner_sum = jnp.sum(probs * grad_probs, axis=-1, keepdims=True)
        score_low = (probs * (grad_probs - inner_sum)).astype(jnp.bfloat16)
        grad_query = (
            jnp.einsum("hqk,khd->qhd", score_low, slot_keys, preferred_element_type=jnp.float32)
            * score_scale
        )
        key_sum = (
            key_sum
            + jnp.einsum("hqk,qhd->khd", score_low, query_part, preferred_element_type=jnp.float32)
            * score_scale
        )
        value_sum = value_sum + jnp.einsum(
            "hqk,qhd->khd",
            probs.astype(jnp.bfloat16),
            grad_part,
            preferred_element_type=jnp.float32,
        )
        return ((key_sum, value_sum), grad_query)

    zero_slab = jnp.zeros((SLOT, heads_here, HEAD_DIM), jnp.float32)
    (key_sum, value_sum), grad_query_blocks = lax.scan(
        backward_block, (zero_slab, zero_slab), (query_blocks, grad_blocks, lse_blocks)
    )
    key_grad_slab = key_sum.reshape(shard_count, tok_rows, width_here)
    value_grad_slab = value_sum.reshape(shard_count, tok_rows, width_here)
    grad_key = jnp.sum(jnp.where(own_hit, key_grad_slab, 0.0), axis=0)
    grad_value = jnp.sum(jnp.where(own_hit, value_grad_slab, 0.0), axis=0)
    for step_by in offset_list:
        far_hit = (spot_ids == my_spot - step_by)[:, None, None]
        send_key = jnp.sum(jnp.where(far_hit, key_grad_slab, 0.0), axis=0)
        send_value = jnp.sum(jnp.where(far_hit, value_grad_slab, 0.0), axis=0)
        back_key_rows, back_value_rows = (
            passed_along(send_key.astype(jnp.bfloat16), "dp", -step_by).astype(send_key.dtype),
            passed_along(send_value.astype(jnp.bfloat16), "dp", -step_by).astype(send_value.dtype),
        )
        grad_key = grad_key + back_key_rows
        grad_value = grad_value + back_value_rows
    query_low = grad_query_blocks.reshape(tok_rows, width_here).astype(jnp.bfloat16)
    key_low = grad_key.astype(jnp.bfloat16)
    value_low = grad_value.astype(jnp.bfloat16)
    grad_w_query = jnp.einsum("td,tc->dc", tokens, query_low, preferred_element_type=jnp.float32)
    grad_w_key = jnp.einsum("td,tc->dc", tokens, key_low, preferred_element_type=jnp.float32)
    grad_w_value = jnp.einsum("td,tc->dc", tokens, value_low, preferred_element_type=jnp.float32)
    grad_b_query = jnp.sum(query_low.astype(jnp.float32), axis=0)
    grad_b_value = jnp.sum(value_low.astype(jnp.float32), axis=0)
    input_part = jnp.einsum("tc,dc->td", query_low, back_query, preferred_element_type=jnp.float32)
    input_part = input_part + jnp.einsum(
        "tc,dc->td", key_low, back_key, preferred_element_type=jnp.float32
    )
    input_part = input_part + jnp.einsum(
        "tc,dc->td", value_low, back_value, preferred_element_type=jnp.float32
    )
    grad_tokens = grad_one + tensor_total(input_part)
    grad_w_query, grad_w_key, grad_w_value, grad_w_out = (
        lax.psum_scatter(
            grad_w_query.astype(jnp.bfloat16), "dp", scatter_dimension=0, tiled=True
        ).astype(jnp.float32),
        lax.psum_scatter(
            grad_w_key.astype(jnp.bfloat16), "dp", scatter_dimension=0, tiled=True
        ).astype(jnp.float32),
        lax.psum_scatter(
            grad_w_value.astype(jnp.bfloat16), "dp", scatter_dimension=0, tiled=True
        ).astype(jnp.float32),
        lax.psum_scatter(
            grad_w_out.astype(jnp.bfloat16), "dp", scatter_dimension=1, tiled=True
        ).astype(jnp.float32),
    )
    (
        grad_b_query,
        grad_b_value,
        grad_b_inner,
        grad_b_out,
        grad_b_outer,
        grad_ln1_gain,
        grad_ln1_bias,
        grad_ln2_gain,
        grad_ln2_bias,
    ) = (
        lax.psum(grad_b_query.astype(jnp.bfloat16), "dp").astype(jnp.float32),
        lax.psum(grad_b_value.astype(jnp.bfloat16), "dp").astype(jnp.float32),
        lax.psum(grad_b_inner.astype(jnp.bfloat16), "dp").astype(jnp.float32),
        lax.psum(grad_b_out.astype(jnp.bfloat16), "dp").astype(jnp.float32),
        lax.psum(grad_b_outer.astype(jnp.bfloat16), "dp").astype(jnp.float32),
        lax.psum(grad_ln1_gain.astype(jnp.bfloat16), "dp").astype(jnp.float32),
        lax.psum(grad_ln1_bias.astype(jnp.bfloat16), "dp").astype(jnp.float32),
        lax.psum(grad_ln2_gain.astype(jnp.bfloat16), "dp").astype(jnp.float32),
        lax.psum(grad_ln2_bias.astype(jnp.bfloat16), "dp").astype(jnp.float32),
    )
    return (
        output,
        grad_tokens,
        grad_w_query,
        grad_w_key,
        grad_w_value,
        grad_b_query,
        grad_b_value,
        grad_w_out,
        grad_b_out,
        grad_ln1_gain,
        grad_ln1_bias,
        grad_w_inner,
        grad_b_inner,
        grad_w_outer,
        grad_b_outer,
        grad_ln2_gain,
        grad_ln2_bias,
    )


def solution(mesh):
    return jax.shard_map(
        on_device,
        mesh=mesh,
        in_specs=(
            P("dp", None),
            P("dp", None),
            P(),
            P(),
            P("dp", "tensor"),
            P("dp", "tensor"),
            P("dp", "tensor"),
            P("tensor"),
            P("tensor"),
            P("tensor", "dp"),
            P(),
            P(),
            P(),
            P("dp", "tensor"),
            P("tensor"),
            P("tensor", "dp"),
            P(),
            P(),
            P(),
        ),
        out_specs=(
            P("dp", None),
            P("dp", None),
            P("dp", "tensor"),
            P("dp", "tensor"),
            P("dp", "tensor"),
            P("tensor"),
            P("tensor"),
            P("tensor", "dp"),
            P(),
            P(),
            P(),
            P("dp", "tensor"),
            P("tensor"),
            P("tensor", "dp"),
            P(),
            P(),
            P(),
        ),
        check_vma=False,
    )
```

profile of v0, /device:TPU:0, one launch (start us, length us, event | category | flops | bytes accessed | tf_op | source)
XLA Modules:
  0.0 1807.7 jit_solution(10736105335624038911)
XLA Ops:
  14.7 27.4 %all-gather.9.cloned.1.call-done = bf16[2048,512]{1,0:T(8,128)(2,1)} async-done(((bf16[256,512]{1,0:T(8,128)(2,1)}), bf16[2048,512]{1,0:T(8,128)(2,1)}) %all-gather.9.cloned.1.call-update) | async-done | bytes 2097168 | tf_op jit(solution)/shard_map/all_gather | solution.py:80
  52.8 25.2 %all-gather.11.cloned.1.call-done = bf16[2048,512]{1,0:T(8,128)(2,1)} async-done(((bf16[256,512]{1,0:T(8,128)(2,1)}), bf16[2048,512]{1,0:T(8,128)(2,1)}) %all-gather.11.cloned.1.call-update) | async-done | bytes 2097168 | tf_op jit(solution)/shard_map/all_gather | solution.py:81
  90.7 26.6 %all-gather.7.cloned.1.call-done = bf16[2048,512]{1,0:T(8,128)(2,1)} async-done(((bf16[256,512]{1,0:T(8,128)(2,1)}), bf16[2048,512]{1,0:T(8,128)(2,1)}) %all-gather.7.cloned.1.call-update) | async-done | bytes 2097168 | tf_op jit(solution)/shard_map/all_gather | solution.py:79
  117.3 6.2 add_convert_fusion.5
  127.6 128.1 %while.31 = (s32[]{:T(128)}, bf16[2,512,4,128]{3,1,2,0:T(8,128)(2,1)}, f32[2,4,512,1]{2,1,3,0:T(4,128)S(1)}, bf16[2,512,4,128]{3,1,2,0:T(8,128)(2,1)}, s32[]{:T(...) while((s32[]{:T(128)}, ...), condition=%wide.region_5.6_spmd.clone.clone, body=%wide.region_2.5_spmd.clone.clone.sunk | while | flops 2204106752 | bytes 137967920 | solution.py:120
  164.7 14.5 select_select_fusion.6
  228.7 14.5 select_select_fusion.6
  258.5 7.3 fusion.74
  271.7 169.3 %all-reduce.6.cloned.1.call-done = f32[1024,2048]{1,0:T(8,128)} async-done(((f32[1024,2048]{1,0:T(8,128)}), f32[1024,2048]{1,0:T(8,128)}) %all-reduce.6.cloned.1.call-update) | async-done | bytes 8388624 | tf_op jit(solution)/shard_map/psum | solution.py:32
  441.0 5.7 fusion.93
  451.1 74.8 %all-gather.15.cloned.1.call-done = bf16[2048,2048]{1,0:T(8,128)(2,1)} async-done(((bf16[256,2048]{1,0:T(8,128)(2,1)}), bf16[2048,2048]{1,0:T(8,128)(2,1)}) %all-gather.15.cloned.1.call-update) | async-done | bytes 8388624 | tf_op jit(solution)/shard_map/all_gather | solution.py:128
  525.9 15.8 fusion.87
  541.7 67.5 %all-gather.17.cloned.1.call-done = bf16[2048,2048]{1,0:T(8,128)(2,1)} async-done(((bf16[2048,256]{1,0:T(8,128)(2,1)}), bf16[2048,2048]{1,0:T(8,128)(2,1)}) %all-gather.17.cloned.1.call-update) | async-done | bytes 8388624 | tf_op jit(solution)/shard_map/all_gather | solution.py:129
  609.2 17.3 fusion.85
  627.5 169.5 %all-reduce.8.cloned.1.call-done = f32[1024,2048]{1,0:T(8,128)} async-done(((f32[1024,2048]{1,0:T(8,128)}), f32[1024,2048]{1,0:T(8,128)}) %all-reduce.8.cloned.1.call-update) | async-done | bytes 8388624 | tf_op jit(solution)/shard_map/psum | solution.py:32
  797.0 7.1 fusion.92
  810.6 7.9 fusion.91
  818.5 23.4 %fusion.94 = (bf16[2048]{0:T(1024)(128)(2,1)}, bf16[1024,2048]{1,0:T(8,128)(2,1)}) fusion(bf16[2048,2048]{1,0:T(8,128)(2,1)} %all-gather.17.cloned.1.call-done, f32[1024,2048]{1,0:T(8,128)} %get-tuple-element.655, f32[1024]{0:T(1024)S(1)} %negate_multiply_fusion.1, f32[1024,2048]{1,0:T(8,128)} %fusion.87, f32[2048]{0:T(1024)S(1)} %copy-done.68), kind=kOutput, calls=%fused_computation.149 | convolution fusion | flops 8648652800 | bytes 29376512 | tf_op jit(solution)/shard_map/td,fd->tf/dot_general | solution.py:145
  842.0 14.5 fusion.95
  856.5 172.9 %all-reduce.10.cloned.1.call-done = f32[1024,2048]{1,0:T(8,128)} async-done(((f32[1024,2048]{1,0:T(8,128)}), f32[1024,2048]{1,0:T(8,128)}) %all-reduce.10.cloned.1.call-update) | async-done | bytes 8388624 | tf_op jit(solution)/shard_map/psum | solution.py:32
  1029.4 11.8 multiply_reduce_fusion.2
  1053.4 6.4 convolution_convert_fusion.6
  1061.4 165.6 %while.32 = (s32[]{:T(128)}, f32[2048,4,128]{0,2,1:T(8,128)}, f32[2048,4,128]{0,2,1:T(8,128)}, bf16[2,512,4,128]{3,1,2,0:T(8,128)(2,1)}, bf16[2,512,4,128]{3,1,2...) while((s32[]{:T(128)}, f32[2048,4,128]{0,2,1:T(8,128)}, ...), condition=%wide.region_19.20_spmd.clone.clone.clone, body=%wide.region_17.19_spmd.clone.clone.clone.sunk | while | flops 5443420160 | bytes 367073888 | solution.py:204
  1082.1 14.4 select_select_fusion.7
  1100.3 5.7 copy-done
  1106.0 5.6 bitcast_add_fusion.5
  1111.6 11.6 multiply_reduce_fusion.8
  1123.2 12.9 multiply_convert_fusion.5
  1163.9 14.4 select_select_fusion.7
  1182.0 5.7 copy-done
  1187.7 7.2 bitcast_add_fusion.5
  1194.9 11.6 multiply_reduce_fusion.8
  1206.5 12.9 multiply_convert_fusion.5
  1230.0 5.9 fusion.67
  1236.0 6.6 reshape.188
  1242.6 6.6 reshape.189
  1249.2 47.1 %select_reduce_fusion.4 = (bf16[1024,512]{0,1:T(8,128)(2,1)}, bf16[1024,512]{0,1:T(8,128)(2,1)}, f32[1024,512]{0,1:T(8,128)S(1)}, f32[1024,512]{0,1:T(8,128)S(1)...) fusion(f32[2,1024,512]{1,0,2:T(2,128)} %reshape.188, pred[2]{0:T(512)(128)(4,1)S(1)} %copy-done.63, ...), kind=kLoop, calls=%fused_computation.97 | loop fusion | flops 9437184 | bytes 16777222 | tf_op jit(solution)/shard_map/reduce_sum | solution.py:213
  1307.3 12.6 collective-permute-start.4
  1328.1 5.9 fusion.68
  1334.2 15.4 convolution_convert_fusion.1
  1350.3 20.0 %convolution_convert_fusion = bf16[2048,2048]{1,0:T(8,128)(2,1)} fusion(f32[1024,2048]{1,0:T(8,128)} %get-tuple-element.655, f32[1024]{0:T(1024)S(1)} %copy-done.54, f32[1024,2048]{1,0:T(8,128)} %fusion.87, f32[2048]{0:T(1024)S(1)} %copy-done.69), kind=kOutput, calls=%fused_computation.84 | convolution fusion | flops 8619294720 | bytes 25178112 | tf_op jit(solution)/shard_map/tf,td->fd/dot_general | solution.py:144
  1378.2 5.9 add_add_fusion.2
  1391.1 10.2 reduce-scatter.9.cloned.1.call-done
  1403.1 88.7 %reduce-scatter.15.cloned.1.call-done = bf16[256,2048]{1,0:T(8,128)(2,1)} async-done(((bf16[2048,2048]{1,0:T(8,128)(2,1)}), bf16[256,2048]{1,0:T(8,128)(2,1)}) %reduce-scatter.15.cloned.1.call-update) | async-done | bytes 1048592 | tf_op jit(solution)/shard_map/reduce_scatter | solution.py:153
  1494.7 87.5 %reduce-scatter.17.cloned.1.call-done = bf16[2048,256]{1,0:T(8,128)(2,1)} async-done(((bf16[2048,2048]{1,0:T(8,128)(2,1)}), bf16[2048,256]{1,0:T(8,128)(2,1)}) %reduce-scatter.17.cloned.1.call-update) | async-done | bytes 1048592 | tf_op jit(solution)/shard_map/reduce_scatter | solution.py:156
  1584.9 172.1 %all-reduce.12.cloned.1.call-done = f32[1024,2048]{1,0:T(8,128)} async-done(((f32[1024,2048]{1,0:T(8,128)}), f32[1024,2048]{1,0:T(8,128)}) %all-reduce.12.cloned.1.call-update) | async-done | bytes 8388624 | tf_op jit(solution)/shard_map/psum | solution.py:32
  1757.0 10.0 add_reduce_fusion
  1767.0 28.6 %all-reduce = (bf16[512]{0:T(512)(128)(2,1)S(1)}, bf16[512]{0:T(512)(128)(2,1)S(1)}, bf16[2048]{0:T(1024)(128)(2,1)S(1)}, bf16[2048]{0:T(1024)(128)(2,1)S(1)}, b...) all-reduce(bf16[512]{0:T(512)(128)(2,1)S(1)} %bitcast.117, ...), channel_id=1, replica_groups=mesh['dp'=8,'tensor'=4] {'dp'}, use_global_device_ids=true, to_apply=%region_31.32 | all-reduce | flops 15360 | bytes 61440 | tf_op jit(solution)/shard_map/psum | solution.py:262
  (368 shorter events, 281.0 us)
Async XLA Ops:
  7.2 34.8 %all-gather.9.cloned.1.call-start = ((), (), s32[]{:S(2)}) async-start(), calls=%async_computation.7 | async-start | bytes 2359296 | tf_op jit(solution)/shard_map/all_gather | solution.py:80
  9.0 68.9 %all-gather.11.cloned.1.call-start = ((), (), s32[]{:S(2)}) async-start(), calls=%async_computation.8 | async-start | bytes 2359296 | tf_op jit(solution)/shard_map/all_gather | solution.py:81
  10.9 106.4 %all-gather.7.cloned.1.call-start = ((), (), s32[]{:S(2)}) async-start(), calls=%async_computation.6 | async-start | bytes 2359296 | tf_op jit(solution)/shard_map/all_gather | solution.py:79
  12.7 245.8 %all-gather.13.cloned.1.call-start = ((), (), s32[]{:S(2)}) async-start(), calls=%async_computation.9 | async-start | bytes 2359296 | tf_op jit(solution)/shard_map/all_gather | solution.py:82
  14.6 426.4 %all-reduce.6.cloned.1.call-start = ((), (), s32[]{:S(2)}) async-start(), calls=%async_computation.10 | async-start | bytes 16777216 | tf_op jit(solution)/shard_map/psum | solution.py:32
  14.6 63.3 %copy-start.70 = (f32[512]{0:T(512)S(1)}, f32[512]{0:T(512)}, u32[]{:S(2)}) copy-start(f32[512]{0:T(512)} %param.31) | copy-start | bytes 6148
  47.2 42.6 %copy-start.72 = (s32[4]{0:T(128)S(1)}, s32[4]{0:T(128)}, u32[]{:S(2)}) copy-start(s32[4]{0:T(128)} %param.25) | copy-start | bytes 52
  47.2 42.6 %copy-start.73 = (s32[4]{0:T(128)S(1)}, s32[4]{0:T(128)}, u32[]{:S(2)}) copy-start(s32[4]{0:T(128)} %param.26) | copy-start | bytes 52
  47.3 70.1 %copy-start.71 = (f32[512]{0:T(512)S(1)}, f32[512]{0:T(512)}, u32[]{:S(2)}) copy-start(f32[512]{0:T(512)} %param.30) | copy-start | bytes 6148
  47.3 79.2 %collective-permute-start.1 = (bf16[1024,512]{1,0:T(8,128)(2,1)S(1)}, bf16[1024,512]{1,0:T(8,128)(2,1)}, u32[]{:S(2)}, u32[]{:S(2)}) collective-permute-start(bf16[1024,512]{1,0:T(8,128)(2,1)S(1)} %convolution_convert_fusion.7), channel_id=1, source_target_pairs={{4,0},{8,4},{12,8},{16,12},{20,16},{24,20},{28,24},{5,1},{9,5},{13... | collective-permute-start | bytes 3145736 | tf_op jit(solution)/shard_map/ppermute | solution.py:14
  48.7 77.7 %collective-permute-start = (bf16[1024,512]{1,0:T(8,128)(2,1)S(1)}, bf16[1024,512]{1,0:T(8,128)(2,1)}, u32[]{:S(2)}, u32[]{:S(2)}) collective-permute-start(bf16[1024,512]{1,0:T(8,128)(2,1)S(1)} %convolution_convert_fusion.7), channel_id=1, source_target_pairs={{0,4},{4,8},{8,12},{12,16},{16,20},{20,24},{24,28},{1,5},{5,9},{9,... | collective-permute-start | bytes 3145736 | tf_op jit(solution)/shard_map/ppermute | solution.py:14
  83.2 43.3 %collective-permute-start.3 = (bf16[1024,512]{1,0:T(8,128)(2,1)S(1)}, bf16[1024,512]{1,0:T(8,128)(2,1)}, u32[]{:S(2)}, u32[]{:S(2)}) collective-permute-start(bf16[1024,512]{1,0:T(8,128)(2,1)S(1)} %add_convert_fusion.4), channel_id=1, source_target_pairs={{4,0},{8,4},{12,8},{16,12},{20,16},{24,20},{28,24},{5,1},{9,5},{13... | collective-permute-start | bytes 3145736 | tf_op jit(solution)/shard_map/ppermute | solution.py:14
  84.5 42.0 %collective-permute-start.2 = (bf16[1024,512]{1,0:T(8,128)(2,1)S(1)}, bf16[1024,512]{1,0:T(8,128)(2,1)}, u32[]{:S(2)}, u32[]{:S(2)}) collective-permute-start(bf16[1024,512]{1,0:T(8,128)(2,1)S(1)} %add_convert_fusion.4), channel_id=1, source_target_pairs={{0,4},{4,8},{8,12},{12,16},{16,20},{20,24},{24,28},{1,5},{5,9},{9,... | collective-permute-start | bytes 3145736 | tf_op jit(solution)/shard_map/ppermute | solution.py:14
  164.7 14.5 copy-start.14
  255.7 191.0 %copy-start.12 = (bf16[1024,512]{1,0:T(8,128)(2,1)}, bf16[1024,512]{1,0:T(8,128)(2,1)S(1)}, u32[]{:S(2)}) copy-start(bf16[1024,512]{1,0:T(8,128)(2,1)S(1)} %get-tuple-element.1027) | copy-start | bytes 3145732
  265.9 175.1 %copy-start.55 = (f32[2048]{0:T(1024)S(1)}, f32[2048]{0:T(1024)}, u32[]{:S(2)}) copy-start(f32[2048]{0:T(1024)} %param.33) | copy-start | bytes 24580
  265.9 260.0 %all-gather.15.cloned.1.call-start = ((), (), s32[]{:S(2)}) async-start(), calls=%async_computation.11 | async-start | bytes 9437184 | tf_op jit(solution)/shard_map/all_gather | solution.py:128
  268.7 340.5 %all-gather.17.cloned.1.call-start = ((), (), s32[]{:S(2)}) async-start(), calls=%async_computation.12 | async-start | bytes 9437184 | tf_op jit(solution)/shard_map/all_gather | solution.py:129
  271.5 525.5 %all-reduce.8.cloned.1.call-start = ((), (), s32[]{:S(2)}) async-start(), calls=%async_computation.13 | async-start | bytes 16777216 | tf_op jit(solution)/shard_map/psum | solution.py:32
  446.8 79.1 %copy-start.41 = (f32[2048]{0:T(1024)S(1)}, f32[2048]{0:T(1024)}, u32[]{:S(2)}) copy-start(f32[2048]{0:T(1024)} %param.34) | copy-start | bytes 24580
  446.8 79.1 %copy-start.58 = (f32[2048]{0:T(1024)S(1)}, f32[2048]{0:T(1024)}, u32[]{:S(2)}) copy-start(f32[2048]{0:T(1024)} %param.35) | copy-start | bytes 24580
  446.8 594.4 %copy-start.39 = (f32[1024]{0:T(1024)}, f32[1024]{0:T(1024)S(1)}, u32[]{:S(2)}) copy-start(f32[1024]{0:T(1024)S(1)} %broadcast_multiply_fusion.1) | copy-start | bytes 12292
  451.1 590.1 %copy-start.43 = (f32[1024]{0:T(1024)}, f32[1024]{0:T(1024)S(1)}, u32[]{:S(2)}) copy-start(f32[1024]{0:T(1024)S(1)} %fusion.81) | copy-start | bytes 12292
  451.1 158.1 %copy-start.68 = (f32[2048]{0:T(1024)S(1)}, f32[2048]{0:T(1024)}, u32[]{:S(2)}) copy-start(f32[2048]{0:T(1024)} %param.37) | copy-start | bytes 24580
  626.5 170.5 %copy-start.56 = (f32[2048]{0:T(1024)S(1)}, f32[2048]{0:T(1024)}, u32[]{:S(2)}) copy-start(f32[2048]{0:T(1024)} %param.39) | copy-start | bytes 24580
  626.6 402.8 %all-reduce.10.cloned.1.call-start = ((), (), s32[]{:S(2)}) async-start(), calls=%async_computation.14 | async-start | bytes 16777216 | tf_op jit(solution)/shard_map/psum | solution.py:32
  818.5 210.9 %copy-start.53 = (f32[1024]{0:T(1024)}, f32[1024]{0:T(1024)S(1)}, u32[]{:S(2)}) copy-start(f32[1024]{0:T(1024)S(1)} %negate_multiply_fusion.1) | copy-start | bytes 12292
  856.5 529.0 %reduce-scatter.13.cloned.1.call-start = ((), (), s32[]{:S(2)}) async-start(), calls=%async_computation.19 | async-start | bytes 2359296 | tf_op jit(solution)/shard_map/reduce_scatter | solution.py:247
  1060.2 327.1 %reduce-scatter.7.cloned.1.call-start = ((), (), s32[]{:S(2)}) async-start(), calls=%async_computation.16 | async-start | bytes 2359296 | tf_op jit(solution)/shard_map/reduce_scatter | solution.py:238
  1082.1 15.8 copy-start.15
  1163.9 15.8 copy-start.15
  1236.0 153.2 %reduce-scatter.11.cloned.1.call-start = ((), (), s32[]{:S(2)}) async-start(), calls=%async_computation.18 | async-start | bytes 2359296 | tf_op jit(solution)/shard_map/reduce_scatter | solution.py:244
  1249.2 54.3 %copy-start.26 = (bf16[1024,2048]{1,0:T(8,128)(2,1)S(1)}, bf16[1024,2048]{1,0:T(8,128)(2,1)}, u32[]{:S(2)}) copy-start(bf16[1024,2048]{1,0:T(8,128)(2,1)} %param.23) | copy-start | bytes 12582916
  1296.3 4.6 collective-permute-start.7
  1297.6 5.5 collective-permute-start.6
  1307.3 94.0 %reduce-scatter.9.cloned.1.call-start = ((), (), s32[]{:S(2)}) async-start(), calls=%async_computation.17 | async-start | bytes 2359296 | tf_op jit(solution)/shard_map/reduce_scatter | solution.py:241
  1307.3 15.0 collective-permute-start.4
  1319.9 6.7 collective-permute-start.5
  1334.1 157.8 %reduce-scatter.15.cloned.1.call-start = ((), (), s32[]{:S(2)}) async-start(), calls=%async_computation.20 | async-start | bytes 9437184 | tf_op jit(solution)/shard_map/reduce_scatter | solution.py:153
  1349.6 232.5 %reduce-scatter.17.cloned.1.call-start = ((), (), s32[]{:S(2)}) async-start(), calls=%async_computation.21 | async-start | bytes 9437184 | tf_op jit(solution)/shard_map/reduce_scatter | solution.py:156
  1370.3 386.7 %all-reduce.12.cloned.1.call-start = ((), (), s32[]{:S(2)}) async-start(), calls=%async_computation.15 | async-start | bytes 16777216 | tf_op jit(solution)/shard_map/psum | solution.py:32
  1384.1 372.9 %copy-start.46 = (f32[1024]{0:T(1024)S(1)}, f32[1024]{0:T(1024)}, u32[]{:S(2)}) copy-start(f32[1024]{0:T(1024)} %copy-done.45) | copy-start | bytes 12292
  1584.8 182.2 %copy-start.48 = (bf16[2048]{0:T(1024)(128)(2,1)S(1)}, bf16[2048]{0:T(1024)(128)(2,1)}, u32[]{:S(2)}) copy-start(bf16[2048]{0:T(1024)(128)(2,1)} %get-tuple-element.565) | copy-start | bytes 12292
  1584.8 182.2 %copy-start.49 = (bf16[2048]{0:T(1024)(128)(2,1)S(1)}, bf16[2048]{0:T(1024)(128)(2,1)}, u32[]{:S(2)}) copy-start(bf16[2048]{0:T(1024)(128)(2,1)} %get-tuple-element.568) | copy-start | bytes 12292
  1584.8 182.2 %copy-start.50 = (bf16[2048]{0:T(1024)(128)(2,1)S(1)}, bf16[2048]{0:T(1024)(128)(2,1)}, u32[]{:S(2)}) copy-start(bf16[2048]{0:T(1024)(128)(2,1)} %get-tuple-element.563) | copy-start | bytes 12292
  1584.8 182.2 %copy-start.51 = (bf16[2048]{0:T(1024)(128)(2,1)S(1)}, bf16[2048]{0:T(1024)(128)(2,1)}, u32[]{:S(2)}) copy-start(bf16[2048]{0:T(1024)(128)(2,1)} %get-tuple-element.567) | copy-start | bytes 12292
  1584.8 182.2 %copy-start.52 = (bf16[2048]{0:T(1024)(128)(2,1)S(1)}, bf16[2048]{0:T(1024)(128)(2,1)}, u32[]{:S(2)}) copy-start(bf16[2048]{0:T(1024)(128)(2,1)} %get-tuple-element.669) | copy-start | bytes 12292
  1584.9 182.2 %copy-start.64 = (bf16[2048]{0:T(1024)(128)(2,1)S(1)}, bf16[2048]{0:T(1024)(128)(2,1)}, u32[]{:S(2)}) copy-start(bf16[2048]{0:T(1024)(128)(2,1)} %get-tuple-element.672) | copy-start | bytes 12292
  (69 other events, 367.9 us)
Sparse Core Ops, SparseCore 0:
  10.2 31.7 all-gather.8
  44.2 33.7 all-gather.10
  80.1 37.1 all-gather.6
  119.3 33.6 all-gather.12
  266.0 174.9 all-reduce.5
  443.1 82.7 all-gather.14
  528.1 81.0 all-gather.16
  626.7 170.2 all-reduce.7
  856.6 172.7 all-reduce.9
  1060.3 36.5 reduce-scatter.12
  1236.1 36.5 reduce-scatter.6
  1307.4 52.8 reduce-scatter.10
  1363.2 37.9 reduce-scatter.8
  1403.5 88.3 reduce-scatter.14
  1494.1 87.9 reduce-scatter.16
  1586.5 170.4 all-reduce.11
where the time goes:
time: 1810 us
  waiting for transfers between devices  1100 us (61%)
  matrix products  235 us (13%)
  other arithmetic  222 us (12%)
  local copies, waits for them, and re-layouts  176 us (10%)
  starting transfers between devices  30.5 us (2%)
  blocking collectives  28.6 us (2%)
    psum x4, waiting for transfers between devices, tensor_total(): return lax.psum(part, 'tensor')  684 us
    reduce_scatter x1, waiting for transfers between devices, on_device(): lax.psum_scatter(grad_w_inner.astype(jnp.bfloat16), 'dp', scatter_dimensi...  88.7 us
    reduce_scatter x1, waiting for transfers between devices, on_device(): lax.psum_scatter(grad_w_outer.astype(jnp.bfloat16), 'dp', scatter_dimensi...  87.5 us
    all_gather x1, waiting for transfers between devices, on_device(): lax.all_gather(w_inner.astype(jnp.bfloat16), 'dp', axis=0, tiled=True)  74.8 us
    all_gather x1, waiting for transfers between devices, on_device(): lax.all_gather(w_outer.astype(jnp.bfloat16), 'dp', axis=1, tiled=True)  67.5 us
    select_n x4, other arithmetic, on_device(): key_slab = jnp.where(far_hit, far_key[None], key_slab)  57.8 us
    dot_general x6, matrix products, mat_bf(): return jnp.dot(left, right, preferred_element_type=jnp.float32)  57 us
    reduce_sum x1, other arithmetic, on_device(): send_key = jnp.sum(jnp.where(far_hit, key_grad_slab, 0.0), axis=0)  47.1 us
  transfers between devices with their start and end apart: 24, of which 15 were waited for; matrix products, arithmetic and copies ran while one was open for 26% of the time, Pallas kernels for 0%

commit v1 on v0

--- a/solution.py
+++ b/solution.py
@@ -6,6 +6,36 @@
 HEAD_DIM = 128
 SLOT = 2048
 norm_eps = 1e-12
+
+
+def write_patches(mat, comm_axis):
+    block_now, block_next, work_now = (
+        lax.axis_size(comm_axis),
+        lax.axis_index(comm_axis),
+        mat.shape[0],
+    )
+    pages = tuple((to_i * block_now if u == 0 else to_i for u, to_i in enumerate(mat.shape)))
+    taken_in = lax.dynamic_update_slice_in_dim(
+        jnp.zeros(pages, mat.dtype), mat, block_next * work_now, axis=0
+    )
+    z_new = arr_now = mat
+    dev_i = 1
+    while dev_i < block_now // 2 + 1:
+        z_new = lax.ppermute(
+            z_new, comm_axis, tuple(((u, (u + 1) % block_now) for u in range(block_now)))
+        )
+        taken_in = lax.dynamic_update_slice_in_dim(
+            taken_in, z_new, (block_next - dev_i) % block_now * work_now, axis=0
+        )
+        if 2 * dev_i < block_now:
+            arr_now = lax.ppermute(
+                arr_now, comm_axis, tuple(((u, (u - 1) % block_now) for u in range(block_now)))
+            )
+            taken_in = lax.dynamic_update_slice_in_dim(
+                taken_in, arr_now, (block_next + dev_i) % block_now * work_now, axis=0
+            )
+        dev_i += 1
+    return taken_in
 
 
 def passed_along(value, axis, steps):
@@ -125,7 +155,7 @@
     hidden, norm_one_back = jax.vjp(layer_norm, resid_one, ln1_gain, ln1_bias)
     hidden_low = hidden.astype(jnp.bfloat16)
     full_inner, full_outer = (
-        lax.all_gather(w_inner.astype(jnp.bfloat16), "dp", axis=0, tiled=True),
+        write_patches(w_inner.astype(jnp.bfloat16), "dp"),
         lax.all_gather(w_outer.astype(jnp.bfloat16), "dp", axis=1, tiled=True),
     )
     inner = mat_bf(hidden_low, full_inner) + b_inner

time: 1810 us -> 1770 us (0.978)
  waiting for transfers between devices: 1100 us -> 1010 us
  starting transfers between devices: 30.5 us -> 56.8 us
    psum x4, waiting for transfers between devices: 684 us -> 592 us  [tensor_total(): return lax.psum(part, 'tensor')]
    ppermute x0 -> x7, waiting for transfers between devices: none -> 46.9 us  [the longest x4 45.6 us: write_patches(): lax.ppermute(z_new, comm_axis, tuple(((u, (u + 1) % block_now) for u in r...]
    all_gather x1, waiting for transfers between devices: 74.8 us -> 38.9 us  [on_device(): lax.all_gather(w_inner.astype(jnp.bfloat16), 'dp', axis=0, tiled=True)]
    ppermute x0 -> x7, starting transfers between devices: none -> 26.4 us  [the longest x4 15.8 us: write_patches(): lax.ppermute(z_new, comm_axis, tuple(((u, (u + 1) % block_now) for u in r...]
  transfers between devices with their start and end apart: 24 -> 31, of which waited for: 15 -> 20; matrix products, arithmetic and copies ran while one was open for 26% -> 30% of each run, Pallas kernels for 0% -> 0%
where the time goes in v1:
time: 1770 us; the launch traced here: 1760 us
  waiting for transfers between devices  1010 us (57%)
  matrix products  234 us (13%)
  other arithmetic  220 us (12%)
  local copies, waits for them, and re-layouts  192 us (11%)
  starting transfers between devices  56.8 us (3%)
  blocking collectives  28.6 us (2%)
    psum x4, waiting for transfers between devices, tensor_total(): return lax.psum(part, 'tensor')  592 us
    reduce_scatter x1, waiting for transfers between devices, on_device(): lax.psum_scatter(grad_w_inner.astype(jnp.bfloat16), 'dp', scatter_dimensi...  88.6 us
    reduce_scatter x1, waiting for transfers between devices, on_device(): lax.psum_scatter(grad_w_outer.astype(jnp.bfloat16), 'dp', scatter_dimensi...  87.4 us
    all_gather x1, waiting for transfers between devices, on_device(): lax.all_gather(w_outer.astype(jnp.bfloat16), 'dp', axis=1, tiled=True)  62.4 us
    select_n x4, other arithmetic, on_device(): key_slab = jnp.where(far_hit, far_key[None], key_slab)  57.8 us
    dot_general x6, matrix products, mat_bf(): return jnp.dot(left, right, preferred_element_type=jnp.float32)  55.4 us
    reduce_sum x1, other arithmetic, on_device(): send_key = jnp.sum(jnp.where(far_hit, key_grad_slab, 0.0), axis=0)  47 us
    ppermute x4, waiting for transfers between devices, write_patches(): lax.ppermute(z_new, comm_axis, tuple(((u, (u + 1) % block_now) for u in r...  45.6 us
  transfers between devices with their start and end apart: 31, of which 20 were waited for; matrix products, arithmetic and copies ran while one was open for 30% of the time, Pallas kernels for 0%

profile of v1, /device:TPU:0, one launch (start us, length us, event | category | flops | bytes accessed | tf_op | source)
XLA Modules:
  0.0 1762.6 jit_solution(12653273118603010585)
XLA Ops:
  14.7 27.4 %all-gather.9.cloned.1.call-done = bf16[2048,512]{1,0:T(8,128)(2,1)} async-done(((bf16[256,512]{1,0:T(8,128)(2,1)}), bf16[2048,512]{1,0:T(8,128)(2,1)}) %all-gather.9.cloned.1.call-update) | async-done | bytes 2097168 | tf_op jit(solution)/shard_map/all_gather | solution.py:110
  52.7 25.2 %all-gather.11.cloned.1.call-done = bf16[2048,512]{1,0:T(8,128)(2,1)} async-done(((bf16[256,512]{1,0:T(8,128)(2,1)}), bf16[2048,512]{1,0:T(8,128)(2,1)}) %all-gather.11.cloned.1.call-update) | async-done | bytes 2097168 | tf_op jit(solution)/shard_map/all_gather | solution.py:111
  90.8 26.6 %all-gather.7.cloned.1.call-done = bf16[2048,512]{1,0:T(8,128)(2,1)} async-done(((bf16[256,512]{1,0:T(8,128)(2,1)}), bf16[2048,512]{1,0:T(8,128)(2,1)}) %all-gather.7.cloned.1.call-update) | async-done | bytes 2097168 | tf_op jit(solution)/shard_map/all_gather | solution.py:109
  117.4 6.2 add_convert_fusion.5
  127.7 128.2 %while.31 = (s32[]{:T(128)}, bf16[2,512,4,128]{3,1,2,0:T(8,128)(2,1)}, f32[2,4,512,1]{2,1,3,0:T(4,128)S(1)}, bf16[2,512,4,128]{3,1,2,0:T(8,128)(2,1)}, s32[]{:T(...) while((s32[]{:T(128)}, ...), condition=%wide.region_5.6_spmd.clone.clone, body=%wide.region_2.5_spmd.clone.clone.sunk | while | flops 2204106752 | bytes 137967920 | solution.py:150
  164.8 14.5 select_select_fusion.6
  228.9 14.5 select_select_fusion.6
  258.8 7.7 fusion.74
  278.6 20.0 %collective-permute-done.4 = bf16[256,2048]{1,0:T(8,128)(2,1)S(1)} collective-permute-done((bf16[256,2048]{1,0:T(8,128)(2,1)S(1)}, bf16[256,2048]{1,0:T(8,128)(2,1)S(1)}, u32[]{:S(2)}, u32[]{:S(2)}) %collective-permute-start.4) | collective-permute-done | bytes 1048608 | tf_op jit(solution)/shard_map/ppermute | solution.py:24
  305.5 15.1 collective-permute-done.6
  333.9 8.6 collective-permute-done.8
  342.5 6.3 collective-permute-start.10
  360.8 80.8 %all-reduce.6.cloned.1.call-done = f32[1024,2048]{1,0:T(8,128)} async-done(((f32[1024,2048]{1,0:T(8,128)}), f32[1024,2048]{1,0:T(8,128)}) %all-reduce.6.cloned.1.call-update) | async-done | bytes 8388624 | tf_op jit(solution)/shard_map/psum | solution.py:62
  450.5 13.9 fusion.87
  464.4 62.4 %all-gather.15.cloned.1.call-done = bf16[2048,2048]{1,0:T(8,128)(2,1)} async-done(((bf16[2048,256]{1,0:T(8,128)(2,1)}), bf16[2048,2048]{1,0:T(8,128)(2,1)}) %all-gather.15.cloned.1.call-update) | async-done | bytes 8388624 | tf_op jit(solution)/shard_map/all_gather | solution.py:159
  526.8 17.3 fusion.85
  545.8 168.9 %all-reduce.8.cloned.1.call-done = f32[1024,2048]{1,0:T(8,128)} async-done(((f32[1024,2048]{1,0:T(8,128)}), f32[1024,2048]{1,0:T(8,128)}) %all-reduce.8.cloned.1.call-update) | async-done | bytes 8388624 | tf_op jit(solution)/shard_map/psum | solution.py:62
  714.6 7.2 fusion.92
  728.5 7.9 fusion.91
  736.4 23.8 %fusion.94 = (bf16[2048]{0:T(1024)(128)(2,1)}, bf16[1024,2048]{1,0:T(8,128)(2,1)}) fusion(bf16[2048,2048]{1,0:T(8,128)(2,1)} %all-gather.15.cloned.1.call-done, f32[1024,2048]{1,0:T(8,128)} %get-tuple-element.655, f32[1024]{0:T(1024)S(1)} %negate_multiply_fusion.1, f32[1024,2048]{1,0:T(8,128)} %fusion.87, f32[2048]{0:T(1024)S(1)} %copy-done.73), kind=kOutput, calls=%fused_computation.157 | convolution fusion | flops 8648652800 | bytes 29376512 | tf_op jit(solution)/shard_map/td,fd->tf/dot_general | solution.py:175
  760.1 38.9 %all-gather.17.cloned.1.call-done = bf16[2048,2048]{1,0:T(8,128)(2,1)} async-done(((bf16[256,2048]{1,0:T(8,128)(2,1)}), bf16[2048,2048]{1,0:T(8,128)(2,1)}) %all-gather.17.cloned.1.call-update) | async-done | bytes 8388624 | tf_op jit(solution)/shard_map/all_gather | solution.py:169
  799.0 14.6 fusion.95
  813.7 170.7 %all-reduce.10.cloned.1.call-done = f32[1024,2048]{1,0:T(8,128)} async-done(((f32[1024,2048]{1,0:T(8,128)}), f32[1024,2048]{1,0:T(8,128)}) %all-reduce.10.cloned.1.call-update) | async-done | bytes 8388624 | tf_op jit(solution)/shard_map/psum | solution.py:62
  984.4 11.5 multiply_reduce_fusion.2
  1008.4 6.4 convolution_convert_fusion.6
  1016.4 165.6 %while.32 = (s32[]{:T(128)}, f32[2048,4,128]{0,2,1:T(8,128)}, f32[2048,4,128]{0,2,1:T(8,128)}, bf16[2,512,4,128]{3,1,2,0:T(8,128)(2,1)}, bf16[2,512,4,128]{3,1,2...) while((s32[]{:T(128)}, f32[2048,4,128]{0,2,1:T(8,128)}, ...), condition=%wide.region_19.20_spmd.clone.clone.clone, body=%wide.region_17.19_spmd.clone.clone.clone.sunk | while | flops 5443420160 | bytes 367073888 | solution.py:234
  1037.2 14.4 select_select_fusion.7
  1066.7 11.6 multiply_reduce_fusion.8
  1078.3 12.9 multiply_convert_fusion.5
  1118.9 14.4 select_select_fusion.7
  1142.8 7.2 bitcast_add_fusion.5
  1150.0 11.6 multiply_reduce_fusion.8
  1161.6 12.9 multiply_convert_fusion.5
  1184.9 5.9 fusion.67
  1190.9 6.6 reshape.188
  1197.5 6.6 reshape.189
  1204.1 47.0 %select_reduce_fusion.4 = (bf16[1024,512]{0,1:T(8,128)(2,1)}, bf16[1024,512]{0,1:T(8,128)(2,1)}, f32[1024,512]{0,1:T(8,128)S(1)}, f32[1024,512]{0,1:T(8,128)S(1)...) fusion(f32[2,1024,512]{1,0,2:T(2,128)} %reshape.188, pred[2]{0:T(512)(128)(4,1)S(1)} %copy-done.68, ...), kind=kLoop, calls=%fused_computation.97 | loop fusion | flops 9437184 | bytes 16777222 | tf_op jit(solution)/shard_map/reduce_sum | solution.py:243
  1262.4 12.6 collective-permute-start.11
  1283.2 5.9 fusion.68
  1289.2 15.4 convolution_convert_fusion.1
  1305.4 20.0 %convolution_convert_fusion = bf16[2048,2048]{1,0:T(8,128)(2,1)} fusion(f32[1024,2048]{1,0:T(8,128)} %get-tuple-element.655, f32[1024]{0:T(1024)S(1)} %copy-done.59, f32[1024,2048]{1,0:T(8,128)} %fusion.87, f32[2048]{0:T(1024)S(1)} %copy-done.74), kind=kOutput, calls=%fused_computation.84 | convolution fusion | flops 8619294720 | bytes 25178112 | tf_op jit(solution)/shard_map/tf,td->fd/dot_general | solution.py:174
  1333.4 5.9 add_add_fusion.2
  1346.2 10.1 reduce-scatter.9.cloned.1.call-done
  1358.2 88.6 %reduce-scatter.15.cloned.1.call-done = bf16[256,2048]{1,0:T(8,128)(2,1)} async-done(((bf16[2048,2048]{1,0:T(8,128)(2,1)}), bf16[256,2048]{1,0:T(8,128)(2,1)}) %reduce-scatter.15.cloned.1.call-update) | async-done | bytes 1048592 | tf_op jit(solution)/shard_map/reduce_scatter | solution.py:183
  1449.6 87.4 %reduce-scatter.17.cloned.1.call-done = bf16[2048,256]{1,0:T(8,128)(2,1)} async-done(((bf16[2048,2048]{1,0:T(8,128)(2,1)}), bf16[2048,256]{1,0:T(8,128)(2,1)}) %reduce-scatter.17.cloned.1.call-update) | async-done | bytes 1048592 | tf_op jit(solution)/shard_map/reduce_scatter | solution.py:186
  1539.8 172.2 %all-reduce.12.cloned.1.call-done = f32[1024,2048]{1,0:T(8,128)} async-done(((f32[1024,2048]{1,0:T(8,128)}), f32[1024,2048]{1,0:T(8,128)}) %all-reduce.12.cloned.1.call-update) | async-done | bytes 8388624 | tf_op jit(solution)/shard_map/psum | solution.py:62
  1711.9 10.0 add_reduce_fusion
  1722.0 28.6 %all-reduce = (bf16[512]{0:T(512)(128)(2,1)S(1)}, bf16[512]{0:T(512)(128)(2,1)S(1)}, bf16[2048]{0:T(1024)(128)(2,1)S(1)}, bf16[2048]{0:T(1024)(128)(2,1)S(1)}, b...) all-reduce(bf16[512]{0:T(512)(128)(2,1)S(1)} %bitcast.117, ...), channel_id=1, replica_groups=mesh['dp'=8,'tensor'=4] {'dp'}, use_global_device_ids=true, to_apply=%region_31.32 | all-reduce | flops 15360 | bytes 61440 | tf_op jit(solution)/shard_map/psum | solution.py:292
  (400 shorter events, 342.4 us)
Async XLA Ops:
  7.2 34.8 %all-gather.9.cloned.1.call-start = ((), (), s32[]{:S(2)}) async-start(), calls=%async_computation.7 | async-start | bytes 2359296 | tf_op jit(solution)/shard_map/all_gather | solution.py:110
  9.0 68.9 %all-gather.11.cloned.1.call-start = ((), (), s32[]{:S(2)}) async-start(), calls=%async_computation.8 | async-start | bytes 2359296 | tf_op jit(solution)/shard_map/all_gather | solution.py:111
  10.9 106.5 %all-gather.7.cloned.1.call-start = ((), (), s32[]{:S(2)}) async-start(), calls=%async_computation.6 | async-start | bytes 2359296 | tf_op jit(solution)/shard_map/all_gather | solution.py:109
  12.7 246.0 %all-gather.13.cloned.1.call-start = ((), (), s32[]{:S(2)}) async-start(), calls=%async_computation.9 | async-start | bytes 2359296 | tf_op jit(solution)/shard_map/all_gather | solution.py:112
  14.6 426.9 %all-reduce.6.cloned.1.call-start = ((), (), s32[]{:S(2)}) async-start(), calls=%async_computation.10 | async-start | bytes 16777216 | tf_op jit(solution)/shard_map/psum | solution.py:62
  14.6 63.3 %copy-start.75 = (f32[512]{0:T(512)S(1)}, f32[512]{0:T(512)}, u32[]{:S(2)}) copy-start(f32[512]{0:T(512)} %param.31) | copy-start | bytes 6148
  47.3 70.2 %copy-start.76 = (f32[512]{0:T(512)S(1)}, f32[512]{0:T(512)}, u32[]{:S(2)}) copy-start(f32[512]{0:T(512)} %param.30) | copy-start | bytes 6148
  47.3 79.3 %collective-permute-start.1 = (bf16[1024,512]{1,0:T(8,128)(2,1)S(1)}, bf16[1024,512]{1,0:T(8,128)(2,1)}, u32[]{:S(2)}, u32[]{:S(2)}) collective-permute-start(bf16[1024,512]{1,0:T(8,128)(2,1)S(1)} %convolution_convert_fusion.7), channel_id=1, source_target_pairs={{4,0},{8,4},{12,8},{16,12},{20,16},{24,20},{28,24},{5,1},{9,5},{13... | collective-permute-start | bytes 3145736 | tf_op jit(solution)/shard_map/ppermute | solution.py:44
  48.7 77.8 %collective-permute-start = (bf16[1024,512]{1,0:T(8,128)(2,1)S(1)}, bf16[1024,512]{1,0:T(8,128)(2,1)}, u32[]{:S(2)}, u32[]{:S(2)}) collective-permute-start(bf16[1024,512]{1,0:T(8,128)(2,1)S(1)} %convolution_convert_fusion.7), channel_id=1, source_target_pairs={{0,4},{4,8},{8,12},{12,16},{16,20},{20,24},{24,28},{1,5},{5,9},{9,... | collective-permute-start | bytes 3145736 | tf_op jit(solution)/shard_map/ppermute | solution.py:44
  83.2 43.4 %collective-permute-start.3 = (bf16[1024,512]{1,0:T(8,128)(2,1)S(1)}, bf16[1024,512]{1,0:T(8,128)(2,1)}, u32[]{:S(2)}, u32[]{:S(2)}) collective-permute-start(bf16[1024,512]{1,0:T(8,128)(2,1)S(1)} %add_convert_fusion.4), channel_id=1, source_target_pairs={{4,0},{8,4},{12,8},{16,12},{20,16},{24,20},{28,24},{5,1},{9,5},{13... | collective-permute-start | bytes 3145736 | tf_op jit(solution)/shard_map/ppermute | solution.py:44
  84.5 42.1 %collective-permute-start.2 = (bf16[1024,512]{1,0:T(8,128)(2,1)S(1)}, bf16[1024,512]{1,0:T(8,128)(2,1)}, u32[]{:S(2)}, u32[]{:S(2)}) collective-permute-start(bf16[1024,512]{1,0:T(8,128)(2,1)S(1)} %add_convert_fusion.4), channel_id=1, source_target_pairs={{0,4},{4,8},{8,12},{12,16},{16,20},{20,24},{24,28},{1,5},{5,9},{9,... | collective-permute-start | bytes 3145736 | tf_op jit(solution)/shard_map/ppermute | solution.py:44
  255.9 100.9 %copy-start.12 = (bf16[1024,512]{1,0:T(8,128)(2,1)}, bf16[1024,512]{1,0:T(8,128)(2,1)S(1)}, u32[]{:S(2)}) copy-start(bf16[1024,512]{1,0:T(8,128)(2,1)S(1)} %get-tuple-element.1029) | copy-start | bytes 3145732
  266.5 260.3 %all-gather.15.cloned.1.call-start = ((), (), s32[]{:S(2)}) async-start(), calls=%async_computation.11 | async-start | bytes 9437184 | tf_op jit(solution)/shard_map/all_gather | solution.py:159
  269.3 445.3 %all-reduce.8.cloned.1.call-start = ((), (), s32[]{:S(2)}) async-start(), calls=%async_computation.12 | async-start | bytes 16777216 | tf_op jit(solution)/shard_map/psum | solution.py:62
  275.0 172.2 %copy-start.24 = (bf16[256,2048]{1,0:T(8,128)(2,1)}, bf16[256,2048]{1,0:T(8,128)(2,1)S(1)}, u32[]{:S(2)}) copy-start(bf16[256,2048]{1,0:T(8,128)(2,1)S(1)} %get-tuple-element.661) | copy-start | bytes 3145732
  275.0 166.5 %copy-start.60 = (f32[2048]{0:T(1024)S(1)}, f32[2048]{0:T(1024)}, u32[]{:S(2)}) copy-start(f32[2048]{0:T(1024)} %param.33) | copy-start | bytes 24580
  275.0 23.5 %collective-permute-start.4 = (bf16[256,2048]{1,0:T(8,128)(2,1)S(1)}, bf16[256,2048]{1,0:T(8,128)(2,1)S(1)}, u32[]{:S(2)}, u32[]{:S(2)}) collective-permute-start(bf16[256,2048]{1,0:T(8,128)(2,1)S(1)} %get-tuple-element.661), channel_id=1, source_target_pairs={{0,4},{4,8},{8,12},{12,16},{16,20},{20,24},{24,28},{28,0},{1,5},{5... | collective-permute-start | bytes 3145736 | tf_op jit(solution)/shard_map/ppermute | solution.py:24
  275.2 27.0 %collective-permute-start.5 = (bf16[256,2048]{1,0:T(8,128)(2,1)S(1)}, bf16[256,2048]{1,0:T(8,128)(2,1)S(1)}, u32[]{:S(2)}, u32[]{:S(2)}) collective-permute-start(bf16[256,2048]{1,0:T(8,128)(2,1)S(1)} %get-tuple-element.661), channel_id=1, source_target_pairs={{0,28},{4,0},{8,4},{12,8},{16,12},{20,16},{24,20},{28,24},{1,29},{... | collective-permute-start | bytes 3145736 | tf_op jit(solution)/shard_map/ppermute | solution.py:31
  298.5 22.1 %collective-permute-start.6 = (bf16[256,2048]{1,0:T(8,128)(2,1)S(1)}, bf16[256,2048]{1,0:T(8,128)(2,1)}, u32[]{:S(2)}, u32[]{:S(2)}) collective-permute-start(bf16[256,2048]{1,0:T(8,128)(2,1)S(1)} %collective-permute-done.4), channel_id=1, source_target_pairs={{0,4},{4,8},{8,12},{12,16},{16,20},{20,24},{24,28},{28,0},{1,5},{5... | collective-permute-start | bytes 3145736 | tf_op jit(solution)/shard_map/ppermute | solution.py:24
  302.3 25.4 %collective-permute-start.7 = (bf16[256,2048]{1,0:T(8,128)(2,1)S(1)}, bf16[256,2048]{1,0:T(8,128)(2,1)}, u32[]{:S(2)}, u32[]{:S(2)}) collective-permute-start(bf16[256,2048]{1,0:T(8,128)(2,1)S(1)} %collective-permute-done.5), channel_id=1, source_target_pairs={{0,28},{4,0},{8,4},{12,8},{16,12},{20,16},{24,20},{28,24},{1,29},{... | collective-permute-start | bytes 3145736 | tf_op jit(solution)/shard_map/ppermute | solution.py:31
  320.7 21.8 %collective-permute-start.8 = (bf16[256,2048]{1,0:T(8,128)(2,1)}, bf16[256,2048]{1,0:T(8,128)(2,1)}, u32[]{:S(2)}, u32[]{:S(2)}) collective-permute-start(bf16[256,2048]{1,0:T(8,128)(2,1)} %collective-permute-done.6), channel_id=1, source_target_pairs={{0,4},{4,8},{8,12},{12,16},{16,20},{20,24},{24,28},{28,0},{1,5},{5... | collective-permute-start | bytes 3145736 | tf_op jit(solution)/shard_map/ppermute | solution.py:24
  327.6 29.2 %collective-permute-start.9 = (bf16[256,2048]{1,0:T(8,128)(2,1)}, bf16[256,2048]{1,0:T(8,128)(2,1)S(1)}, u32[]{:S(2)}, u32[]{:S(2)}) collective-permute-start(bf16[256,2048]{1,0:T(8,128)(2,1)} %collective-permute-done.7), channel_id=1, source_target_pairs={{0,28},{4,0},{8,4},{12,8},{16,12},{20,16},{24,20},{28,24},{1,29},{... | collective-permute-start | bytes 3145736 | tf_op jit(solution)/shard_map/ppermute | solution.py:31
  342.5 17.2 collective-permute-start.10
  447.3 548.7 %copy-start.44 = (f32[1024]{0:T(1024)}, f32[1024]{0:T(1024)S(1)}, u32[]{:S(2)}) copy-start(f32[1024]{0:T(1024)S(1)} %broadcast_multiply_fusion.1) | copy-start | bytes 12292
  450.5 545.4 %copy-start.48 = (f32[1024]{0:T(1024)}, f32[1024]{0:T(1024)S(1)}, u32[]{:S(2)}) copy-start(f32[1024]{0:T(1024)S(1)} %fusion.81) | copy-start | bytes 12292
  450.5 76.3 %copy-start.73 = (f32[2048]{0:T(1024)S(1)}, f32[2048]{0:T(1024)}, u32[]{:S(2)}) copy-start(f32[2048]{0:T(1024)} %param.37) | copy-start | bytes 24580
  544.1 170.5 %copy-start.61 = (f32[2048]{0:T(1024)S(1)}, f32[2048]{0:T(1024)}, u32[]{:S(2)}) copy-start(f32[2048]{0:T(1024)} %param.39) | copy-start | bytes 24580
  544.2 254.8 %all-gather.17.cloned.1.call-start = ((), (), s32[]{:S(2)}) async-start(), calls=%async_computation.13 | async-start | bytes 9437184 | tf_op jit(solution)/shard_map/all_gather | solution.py:169
  544.9 439.5 %all-reduce.10.cloned.1.call-start = ((), (), s32[]{:S(2)}) async-start(), calls=%async_computation.14 | async-start | bytes 16777216 | tf_op jit(solution)/shard_map/psum | solution.py:62
  736.4 248.1 %copy-start.58 = (f32[1024]{0:T(1024)}, f32[1024]{0:T(1024)S(1)}, u32[]{:S(2)}) copy-start(f32[1024]{0:T(1024)S(1)} %negate_multiply_fusion.1) | copy-start | bytes 12292
  813.7 527.0 %reduce-scatter.13.cloned.1.call-start = ((), (), s32[]{:S(2)}) async-start(), calls=%async_computation.19 | async-start | bytes 2359296 | tf_op jit(solution)/shard_map/reduce_scatter | solution.py:277
  1015.2 327.3 %reduce-scatter.7.cloned.1.call-start = ((), (), s32[]{:S(2)}) async-start(), calls=%async_computation.16 | async-start | bytes 2359296 | tf_op jit(solution)/shard_map/reduce_scatter | solution.py:268
  1190.9 153.5 %reduce-scatter.11.cloned.1.call-start = ((), (), s32[]{:S(2)}) async-start(), calls=%async_computation.18 | async-start | bytes 2359296 | tf_op jit(solution)/shard_map/reduce_scatter | solution.py:274
  1251.2 4.8 collective-permute-start.14
  1252.4 5.7 collective-permute-start.13
  1262.4 94.0 %reduce-scatter.9.cloned.1.call-start = ((), (), s32[]{:S(2)}) async-start(), calls=%async_computation.17 | async-start | bytes 2359296 | tf_op jit(solution)/shard_map/reduce_scatter | solution.py:271
  1262.4 15.0 collective-permute-start.11
  1275.0 6.7 collective-permute-start.12
  1289.2 157.7 %reduce-scatter.15.cloned.1.call-start = ((), (), s32[]{:S(2)}) async-start(), calls=%async_computation.20 | async-start | bytes 9437184 | tf_op jit(solution)/shard_map/reduce_scatter | solution.py:183
  1304.7 232.3 %reduce-scatter.17.cloned.1.call-start = ((), (), s32[]{:S(2)}) async-start(), calls=%async_computation.21 | async-start | bytes 9437184 | tf_op jit(solution)/shard_map/reduce_scatter | solution.py:186
  1325.5 386.5 %all-reduce.12.cloned.1.call-start = ((), (), s32[]{:S(2)}) async-start(), calls=%async_computation.15 | async-start | bytes 16777216 | tf_op jit(solution)/shard_map/psum | solution.py:62
  1339.3 372.7 %copy-start.51 = (f32[1024]{0:T(1024)S(1)}, f32[1024]{0:T(1024)}, u32[]{:S(2)}) copy-start(f32[1024]{0:T(1024)} %copy-done.50) | copy-start | bytes 12292
  1539.8 182.2 %copy-start.53 = (bf16[2048]{0:T(1024)(128)(2,1)S(1)}, bf16[2048]{0:T(1024)(128)(2,1)}, u32[]{:S(2)}) copy-start(bf16[2048]{0:T(1024)(128)(2,1)} %get-tuple-element.565) | copy-start | bytes 12292
  1539.8 182.2 %copy-start.54 = (bf16[2048]{0:T(1024)(128)(2,1)S(1)}, bf16[2048]{0:T(1024)(128)(2,1)}, u32[]{:S(2)}) copy-start(bf16[2048]{0:T(1024)(128)(2,1)} %get-tuple-element.568) | copy-start | bytes 12292
  1539.8 182.2 %copy-start.55 = (bf16[2048]{0:T(1024)(128)(2,1)S(1)}, bf16[2048]{0:T(1024)(128)(2,1)}, u32[]{:S(2)}) copy-start(bf16[2048]{0:T(1024)(128)(2,1)} %get-tuple-element.563) | copy-start | bytes 12292
  1539.8 182.2 %copy-start.56 = (bf16[2048]{0:T(1024)(128)(2,1)S(1)}, bf16[2048]{0:T(1024)(128)(2,1)}, u32[]{:S(2)}) copy-start(bf16[2048]{0:T(1024)(128)(2,1)} %get-tuple-element.567) | copy-start | bytes 12292
  1539.8 182.2 %copy-start.57 = (bf16[2048]{0:T(1024)(128)(2,1)S(1)}, bf16[2048]{0:T(1024)(128)(2,1)}, u32[]{:S(2)}) copy-start(bf16[2048]{0:T(1024)(128)(2,1)} %get-tuple-element.671) | copy-start | bytes 12292
  1539.8 182.2 %copy-start.69 = (bf16[2048]{0:T(1024)(128)(2,1)S(1)}, bf16[2048]{0:T(1024)(128)(2,1)}, u32[]{:S(2)}) copy-start(bf16[2048]{0:T(1024)(128)(2,1)} %get-tuple-element.674) | copy-start | bytes 12292
  (81 other events, 587.6 us)
Sparse Core Ops, SparseCore 0:
  10.2 31.7 all-gather.8
  44.2 33.7 all-gather.10
  80.1 37.2 all-gather.6
  119.4 33.6 all-gather.12
  266.6 174.8 all-reduce.5
  443.6 83.1 all-gather.14
  544.3 170.2 all-reduce.7
  716.2 82.7 all-gather.16
  813.8 170.6 all-reduce.9
  1015.3 36.5 reduce-scatter.12
  1191.0 36.5 reduce-scatter.6
  1262.5 52.8 reduce-scatter.10
  1318.3 37.9 reduce-scatter.8
  1358.6 88.2 reduce-scatter.14
  1449.1 87.9 reduce-scatter.16
  1541.4 170.4 all-reduce.11
